TPU v7x, 32 devices: a whole 2x2x4 slice. The times are simulated.
32 devices in a mesh: section: 8 (over y, x, core), dp: 4 (over z).
Axes of the slice: x: 2, y: 2, z: 4, core: 2. Of those that a mesh axis runs over, the one named last changes fastest.
Arguments:
- inputs: bfloat16 [4, 8, 128, 4096], P('dp', 'section'), may hold values from -6 to 6
- key_rows: bfloat16 [4, 8, 24, 4096], P('dp', None, None, 'section'), may hold values from -32 to 32
- value_rows: bfloat16 [4, 8, 24, 4096], P('dp', None, None, 'section'), may hold values from -6 to 6
- query_gain: float32 [8, 4096], P('section'), may hold values from 0.1 to 1.9
- cotangent: bfloat16 [4, 8, 128, 4096], P('dp', 'section'), may hold values from -6 to 6
Outputs:
- key_grads: bfloat16 [4, 8, 24, 4096], P('dp', None, None, 'section')
- value_grads: bfloat16 [4, 8, 24, 4096], P('dp', None, None, 'section')
- gain_grads: float32 [8, 4096], P('section')
All inputs are finite; a program needn't handle non-finite values.
Results may differ from a plain program's by a relative error of at most 0.008.
Values may be sent and summed in bfloat16 or wider, within the bound.
A program may use at most 64 MiB of HBM per device.

v0:
```python
import jax
import jax.numpy as jnp
from jax import lax
from jax.sharding import PartitionSpec as P

HEAD = 64
TICKS = 3


def from_behind(x, axis, by):
    length = lax.axis_size(axis)
    return lax.ppermute(x, axis, [(i, (i + by) % length) for i in range(length)])


def product(form, left, right):
    return jnp.einsum(form, left, right, preferred_element_type=jnp.float32)


def attend_forward(states, gain_row, key_block, value_block):
    floats = states.astype(jnp.float32)
    inverse = lax.rsqrt(jnp.mean(floats * floats, axis=-1, keepdims=True) + 1e-06)
    queries = (floats * inverse * gain_row).astype(jnp.bfloat16)
    tok_rows, width = states.shape
    src_rows = key_block.shape[0]
    heads_count = width // HEAD
    query_heads = queries.reshape(tok_rows, heads_count, HEAD)
    key_heads = key_block.reshape(src_rows, heads_count, HEAD)
    value_heads = value_block.reshape(src_rows, heads_count, HEAD)
    scores = product("shd,thd->hst", key_heads, query_heads) * HEAD ** (-0.5)
    highest = jnp.max(scores, axis=1, keepdims=True)
    weights = jnp.exp(scores - highest)
    probs = weights / jnp.sum(weights, axis=1, keepdims=True)
    probs_low = probs.astype(jnp.bfloat16)
    mixed = product("hst,shd->thd", probs_low, value_heads).reshape(tok_rows, width)
    produced = (floats + mixed).astype(jnp.bfloat16)
    return (produced, (inverse, queries, probs, probs_low))


def attend_backward(states, gain_row, key_block, value_block, saved, incoming, needed):
    inverse, queries, probs, probs_low = saved
    tok_rows, width = states.shape
    src_rows = key_block.shape[0]
    heads_count = width // HEAD
    query_heads = queries.reshape(tok_rows, heads_count, HEAD)
    key_heads = key_block.reshape(src_rows, heads_count, HEAD)
    value_heads = value_block.reshape(src_rows, heads_count, HEAD)
    grad_heads = incoming.reshape(tok_rows, heads_count, HEAD)
    dprob = product("shd,thd->hst", value_heads, grad_heads)
    dscore = (
        probs * (dprob - jnp.sum(probs * dprob, axis=1, keepdims=True)) * HEAD ** (-0.5)
    ).astype(jnp.bfloat16)
    value_step = product("hst,thd->shd", probs_low, grad_heads).reshape(src_rows, width)
    key_step = product("hst,thd->shd", dscore, query_heads).reshape(src_rows, width)
    dquery = product("hst,shd->thd", dscore, key_heads).reshape(tok_rows, width)
    unit = states.astype(jnp.float32) * inverse
    gain_step = jnp.sum(dquery * unit, axis=0)
    if needed:
        scaled = gain_row * dquery
        back = incoming.astype(jnp.float32) + inverse * (
            scaled - unit * jnp.mean(scaled * unit, axis=-1, keepdims=True)
        )
        back = back.astype(jnp.bfloat16)
    else:
        back = None
    return (back, key_step, value_step, gain_step)


def on_device(inputs, key_rows, value_rows, query_gain, cotangent):
    arrived = (
        lax.all_to_all(key_rows, "section", split_axis=1, concat_axis=3, tiled=True),
        lax.all_to_all(value_rows, "section", split_axis=1, concat_axis=3, tiled=True),
    )
    local_keys = arrived[0][0, 0]
    local_values = arrived[1][0, 0]
    gain_row = query_gain[0]
    current = inputs[0, 0]
    states = [current]
    for tick_index in range(TICKS):
        if tick_index + 1 < TICKS:
            produced, saved = attend_forward(current, gain_row, local_keys, local_values)
        if tick_index + 1 < TICKS:
            current = from_behind(produced, "section", 1)
            states.append(current)
    key_total = jnp.zeros(local_keys.shape, jnp.float32)
    value_total = jnp.zeros(local_values.shape, jnp.float32)
    gain_total = jnp.zeros(gain_row.shape, jnp.float32)
    carried = cotangent[0, 0]
    for tick_index in range(TICKS - 1, -1, -1):
        incoming = from_behind(carried, "section", -1)
        saved = attend_forward(states[tick_index], gain_row, local_keys, local_values)[1]
        carried, key_step, value_step, gain_step = attend_backward(
            states[tick_index], gain_row, local_keys, local_values, saved, incoming, tick_index > 0
        )
        key_total = key_total + key_step
        value_total = value_total + value_step
        gain_total = gain_total + gain_step
    returned = (
        lax.all_to_all(
            key_total.astype(jnp.bfloat16)[None, None],
            "section",
            split_axis=3,
            concat_axis=1,
            tiled=True,
        ),
        lax.all_to_all(
            value_total.astype(jnp.bfloat16)[None, None],
            "section",
            split_axis=3,
            concat_axis=1,
            tiled=True,
        ),
    )
    gain_summed = lax.psum(gain_total, "dp")
    return (returned[0], returned[1], gain_summed[None])


def solution(mesh):
    return jax.shard_map(
        on_device,
        mesh=mesh,
        in_specs=(
            P("dp", "section", None, None),
            P("dp", None, None, "section"),
            P("dp", None, None, "section"),
            P("section", None),
            P("dp", "section", None, None),
        ),
        out_specs=(
            P("dp", None, None, "section"),
            P("dp", None, None, "section"),
            P("section", None),
        ),
        check_vma=False,
    )
```

profile of v0, /device:TPU:0, one launch (start us, length us, event | category | flops | bytes accessed | tf_op | source)
XLA Modules:
  0.0 241.4 jit_solution(5786657829530134387)
XLA Ops:
  0.6 5.2 %all-to-all-start = ((bf16[1,8,24,512]{3,2,0,1:T(8,128)(2,1)}), bf16[1,8,24,512]{3,2,0,1:T(8,128)(2,1)S(1)}, u32[]{:S(2)}, u32[]{:S(2)}) async-start(bf16[1,8,24,512]{3,2,0,1:T(8,128)(2,1)} %bitcast.148), calls=%async_computation | async-start | bytes 393216 | tf_op jit(solution)/shard_map/all_to_all | solution.py:70
  12.0 3.4 %all-to-all-start.1 = ((bf16[1,8,24,512]{3,2,0,1:T(8,128)(2,1)}), bf16[1,8,24,512]{3,2,0,1:T(8,128)(2,1)S(1)}, u32[]{:S(2)}, u32[]{:S(2)}) async-start(bf16[1,8,24,512]{3,2,0,1:T(8,128)(2,1)} %bitcast.6), calls=%async_computation.1 | async-start | bytes 393216 | tf_op jit(solution)/shard_map/all_to_all | solution.py:71
  15.5 6.0 %all-to-all-done.1 = bf16[1,8,24,512]{3,2,0,1:T(8,128)(2,1)S(1)} async-done(((bf16[1,8,24,512]{3,2,0,1:T(8,128)(2,1)}), bf16[1,8,24,512]{3,2,0,1:T(8,128)(2,1)S(1)}, u32[]{:S(2)}, u32[]{:S(2)}) %all-to-all-start.1) | async-done | bytes 196640 | tf_op jit(solution)/shard_map/all_to_all | solution.py:71
  32.8 19.4 %collective-permute-done = bf16[128,4096]{0,1:T(8,128)(2,1)S(1)} collective-permute-done((bf16[128,4096]{0,1:T(8,128)(2,1)}, bf16[128,4096]{0,1:T(8,128)(2,1)S(1)}, u32[]{:S(2)}, u32[]{:S(2)}) %collective-permute-start) | collective-permute-done | bytes 1048608 | tf_op jit(solution)/shard_map/ppermute | solution.py:12
  56.5 3.3 %fusion.88 = f32[64,128,64]{1,2,0:T(8,128)} fusion(bf16[24,64,64]{2,1,0:T(8,128)(2,1)S(1)} %reshape_squeeze.5, f32[64,128]{1,0:T(8,128)} %get-tuple-element.15, f32[64,24,128]{2,1,0:T(8,128)} %copy-done.11), kind=kOutput, calls=%fused_computation.108 | convolution fusion | flops 25763864 | bytes 3112960 | tf_op jit(solution)/shard_map/hst,shd->thd/dot_general | solution.py:16
  64.4 12.5 %collective-permute-done.1 = bf16[128,4096]{0,1:T(8,128)(2,1)S(1)} collective-permute-done((bf16[128,4096]{0,1:T(8,128)(2,1)S(1)}, bf16[128,4096]{0,1:T(8,128)(2,1)S(1)}, u32[]{:S(2)}, u32[]{:S(2)}) %collective-permute-start.1) | collective-permute-done | bytes 1048608 | tf_op jit(solution)/shard_map/ppermute | solution.py:12
  82.2 4.0 %fusion.61 = f32[64,128,64]{1,2,0:T(8,128)} fusion(f32[64,24,128]{2,1,0:T(8,128)} %fusion.86, bf16[24,64,64]{2,1,0:T(8,128)(2,1)} %copy-done.6, f32[64,24,128]{2,1,0:T(8,128)} %get-tuple-element.18, f32[64,128]{1,0:T(8,128)} %get-tuple-element.17), kind=kOutput, calls=%fused_computation.81 | convolution fusion | flops 26550296 | bytes 3899392 | tf_op jit(solution)/shard_map/hst,shd->thd/dot_general | solution.py:16
  86.2 3.3 %fusion.20 = (f32[4096]{0:T(1024)}, f32[128]{0:T(128)S(1)}) fusion(bf16[128,4096]{0,1:T(8,128)(2,1)S(1)} %collective-permute-done.1, f32[64,128,64]{1,2,0:T(8,128)} %fusion.61, f32[128]{0:T(128)} %copy-done.23, f32[4096]{0:T(1024)S(1)} %bitcast.138), kind=kLoop, calls=%fused_computation.25 | loop fusion | flops 3665792 | bytes 3179520 | tf_op jit(solution)/shard_map/reduce_sum | solution.py:56
  91.5 12.3 %collective-permute-done.3 = bf16[128,4096]{0,1:T(8,128)(2,1)S(1)} collective-permute-done((bf16[128,4096]{0,1:T(8,128)(2,1)S(1)}, bf16[128,4096]{0,1:T(8,128)(2,1)S(1)}, u32[]{:S(2)}, u32[]{:S(2)}) %collective-permute-start.3) | collective-permute-done | bytes 1048608 | tf_op jit(solution)/shard_map/ppermute | solution.py:12
  105.1 4.0 %fusion.66 = f32[64,128,64]{1,2,0:T(8,128)} fusion(f32[64,24,128]{2,1,0:T(8,128)} %convolution_bitcast_fusion.4, bf16[24,64,64]{2,1,0:T(8,128)(2,1)} %copy-done.6, f32[64,24,128]{2,1,0:T(8,128)} %get-tuple-element.16, f32[64,128]{1,0:T(8,128)} %get-tuple-element.15), kind=kOutput, calls=%fused_computation.85 | convolution fusion | flops 26550296 | bytes 3899392 | tf_op jit(solution)/shard_map/hst,shd->thd/dot_general | solution.py:16
  109.1 3.3 %fusion.28 = (f32[4096]{0:T(1024)}, f32[128]{0:T(128)S(1)}) fusion(bf16[128,4096]{0,1:T(8,128)(2,1)S(1)} %collective-permute-done, f32[64,128,64]{1,2,0:T(8,128)} %fusion.66, f32[128]{0:T(128)} %copy-done.21, f32[4096]{0:T(1024)S(1)} %bitcast.140), kind=kLoop, calls=%fused_computation.33 | loop fusion | flops 3665792 | bytes 3179520 | tf_op jit(solution)/shard_map/reduce_sum | solution.py:56
  117.0 3.0 %convolution_bitcast_fusion.1 = f32[24,64,64]{2,0,1:T(8,128)} fusion(bf16[128,64,64]{0,2,1:T(8,128)(2,1)S(1)} %bitcast.135, f32[64,128]{1,0:T(8,128)} %get-tuple-element.15, f32[64,24,128]{2,1,0:T(8,128)} %copy-done.11), kind=kOutput, calls=%fused_computation.52 | convolution fusion | flops 25763864 | bytes 2260992 | tf_op jit(solution)/shard_map/hst,thd->shd/dot_general | solution.py:16
  119.9 3.4 %fusion.67 = f32[64,64,24]{1,2,0:T(8,128)} fusion(bf16[128,64,64]{0,2,1:T(8,128)(2,1)S(1)} %bitcast.133, f32[64,24,128]{2,1,0:T(8,128)} %convolution_bitcast_fusion.4, f32[64,24,128]{2,1,0:T(8,128)} %get-tuple-element.16, f32[64,128]{1,0:T(8,128)} %get-tuple-element.15), kind=kOutput, calls=%fused_computation.86 | convolution fusion | flops 26550296 | bytes 3047424 | tf_op jit(solution)/shard_map/hst,thd->shd/dot_general | solution.py:16
  123.3 6.2 %collective-permute-done.4 = bf16[128,4096]{0,1:T(8,128)(2,1)} collective-permute-done((bf16[128,4096]{0,1:T(8,128)(2,1)}, bf16[128,4096]{0,1:T(8,128)(2,1)}, u32[]{:S(2)}, u32[]{:S(2)}) %collective-permute-start.4) | collective-permute-done | bytes 1048608 | tf_op jit(solution)/shard_map/ppermute | solution.py:12
  129.6 3.3 %convolution_bitcast_fusion = f32[24,64,64]{2,0,1:T(8,128)} fusion(bf16[128,64,64]{0,2,1:T(8,128)(2,1)} %bitcast.26, f32[64,128]{1,0:T(8,128)S(1)} %copy-done.17, f32[64,24,128]{2,1,0:T(8,128)} %copy-done.14), kind=kOutput, calls=%fused_computation.51 | convolution fusion | flops 25763864 | bytes 2260992 | tf_op jit(solution)/shard_map/hst,thd->shd/dot_general | solution.py:16
  144.2 23.5 %reduce.6 = bf16[4096,24]{1,0:T(8,128)(2,1)} reduce(bf16[4096,1,1,24]{3,2,1,0:T(2,128)(2,1)S(1)} %bitcast.126, bf16[]{:T(256)} %broadcast.122), dimensions={1,2}, to_apply=%bitcast.103.reduce_sub_computation | reduce | bytes 393218
  167.7 3.4 %reshape.199 = bf16[8,2,6144]{2,1,0:T(2,128)(2,1)} reshape(bf16[4096,24]{1,0:T(8,128)(2,1)} %reduce.6) | data formatting | bytes 393216
  171.0 4.1 %all-to-all-start.3 = ((bf16[8,2,6144]{2,1,0:T(2,128)(2,1)}), bf16[8,2,6144]{2,1,0:T(2,128)(2,1)S(1)}, u32[]{:S(2)}, u32[]{:S(2)}) async-start(bf16[8,2,6144]{2,1,0:T(2,128)(2,1)} %reshape.199), calls=%async_computation.3 | async-start | bytes 393216 | tf_op jit(solution)/shard_map/all_to_all | solution.py:105
  175.1 3.0 %fusion.60 = bf16[24,64,64]{2,0,1:T(8,128)(2,1)S(1)} fusion(f32[64,64,24]{1,2,0:T(8,128)} %fusion.72, f32[64,64,24]{1,2,0:T(8,128)} %fusion.67, bf16[128,64,64]{0,2,1:T(8,128)(2,1)S(1)} %bitcast.131, f32[64,24,128]{2,1,0:T(8,128)} %fusion.86, f32[64,24,128]{2,1,0:T(8,128)} %get-tuple-element.18, f32[64,128]{1,0:T(8,128)S(1)} %copy-done.18), kind=kOutput, calls=%fused_computation.80 | convolution fusion | flops 26845208 | bytes 3637248 | tf_op jit(solution)/shard_map/hst,thd->shd/dot_general | solution.py:16
  181.4 22.4 %reduce.5 = bf16[4096,24]{1,0:T(8,128)(2,1)S(1)} reduce(bf16[4096,1,1,24]{3,2,1,0:T(2,128)(2,1)S(1)} %bitcast.127, bf16[]{:T(256)} %broadcast.122), dimensions={1,2}, to_apply=%bitcast.101.reduce_sub_computation | reduce | bytes 393218
  205.8 4.2 %all-to-all-start.2 = ((bf16[8,2,6144]{2,1,0:T(2,128)(2,1)}), bf16[8,2,6144]{2,1,0:T(2,128)(2,1)S(1)}, u32[]{:S(2)}, u32[]{:S(2)}) async-start(bf16[8,2,6144]{2,1,0:T(2,128)(2,1)} %reshape.197), calls=%async_computation.2 | async-start | bytes 393216 | tf_op jit(solution)/shard_map/all_to_all | solution.py:98
  210.0 19.6 %psum.7 = f32[1,4096]{1,0:T(1,128)} all-reduce(f32[1,4096]{1,0:T(1,128)S(1)} %bitcast.149), channel_id=1, replica_groups=mesh['section'=8,'dp'=4] {'dp'}, use_global_device_ids=true, to_apply=%region_17.0 | all-reduce | flops 4096 | bytes 32768 | tf_op jit(solution)/shard_map/psum | solution.py:113
  229.6 3.0 %reshape.200 = bf16[4096,1,1,24]{3,2,1,0:T(2,128)(2,1)S(1)} reshape(bf16[8,2,6144]{2,1,0:T(2,128)(2,1)S(1)} %all-to-all-done.3) | data formatting | bytes 393216
  235.5 3.0 %reshape.198 = bf16[4096,1,1,24]{3,2,1,0:T(2,128)(2,1)S(1)} reshape(bf16[8,2,6144]{2,1,0:T(2,128)(2,1)S(1)} %all-to-all-done.2) | data formatting | bytes 393216
  (115 shorter events, 61.7 us)
Async XLA Ops:
  0.6 11.4 %all-to-all-start = ((bf16[1,8,24,512]{3,2,0,1:T(8,128)(2,1)}), bf16[1,8,24,512]{3,2,0,1:T(8,128)(2,1)S(1)}, u32[]{:S(2)}, u32[]{:S(2)}) async-start(bf16[1,8,24,512]{3,2,0,1:T(8,128)(2,1)} %bitcast.148), calls=%async_computation | async-start | bytes 393216 | tf_op jit(solution)/shard_map/all_to_all | solution.py:70
  7.8 14.3 %copy-start.19 = (f32[64,64]{1,0:T(8,128)}, f32[64,64]{1,0:T(8,128)S(1)}, u32[]{:S(2)}) copy-start(f32[64,64]{1,0:T(8,128)S(1)} %mul.98) | copy-start | bytes 49156
  12.0 9.5 %all-to-all-start.1 = ((bf16[1,8,24,512]{3,2,0,1:T(8,128)(2,1)}), bf16[1,8,24,512]{3,2,0,1:T(8,128)(2,1)S(1)}, u32[]{:S(2)}, u32[]{:S(2)}) async-start(bf16[1,8,24,512]{3,2,0,1:T(8,128)(2,1)} %bitcast.6), calls=%async_computation.1 | async-start | bytes 393216 | tf_op jit(solution)/shard_map/all_to_all | solution.py:71
  15.5 7.4 %copy-start.25 = (f32[128]{0:T(128)}, f32[128]{0:T(128)S(1)}, u32[]{:S(2)}) copy-start(f32[128]{0:T(128)S(1)} %add_rsqrt_fusion.2) | copy-start | bytes 1540
  27.9 24.9 %copy-start.12 = (f32[1,4096]{1,0:T(1,128)S(1)}, f32[1,4096]{1,0:T(1,128)}, u32[]{:S(2)}) copy-start(f32[1,4096]{1,0:T(1,128)} %param.8) | copy-start | bytes 49156
  27.9 24.3 %collective-permute-start = (bf16[128,4096]{0,1:T(8,128)(2,1)}, bf16[128,4096]{0,1:T(8,128)(2,1)S(1)}, u32[]{:S(2)}, u32[]{:S(2)}) collective-permute-start(bf16[128,4096]{0,1:T(8,128)(2,1)} %fusion.31), channel_id=1, source_target_pairs={{0,4},{4,8},{8,12},{12,16},{16,20},{20,24},{24,28},{28,0},{1,5},{5... | collective-permute-start | bytes 3145736 | tf_op jit(solution)/shard_map/ppermute | solution.py:12
  30.2 23.4 %copy-start.7 = (bf16[24,64,64]{2,1,0:T(8,128)(2,1)S(1)}, bf16[24,64,64]{2,1,0:T(8,128)(2,1)}, u32[]{:S(2)}) copy-start(bf16[24,64,64]{2,1,0:T(8,128)(2,1)} %copy-done.6) | copy-start | bytes 589828
  30.2 31.6 %collective-permute-start.2 = (bf16[128,4096]{0,1:T(8,128)(2,1)}, bf16[128,4096]{0,1:T(8,128)(2,1)}, u32[]{:S(2)}, u32[]{:S(2)}) collective-permute-start(bf16[128,4096]{0,1:T(8,128)(2,1)} %bitcast.18), channel_id=1, source_target_pairs={{0,28},{4,0},{8,4},{12,8},{16,12},{20,16},{24,20},{28,24},{1,29},{... | collective-permute-start | bytes 3145736 | tf_op jit(solution)/shard_map/ppermute | solution.py:12
  53.5 6.4 %copy-start.4 = (bf16[128,4096]{0,1:T(8,128)(2,1)}, bf16[128,4096]{0,1:T(8,128)(2,1)S(1)}, u32[]{:S(2)}) copy-start(bf16[128,4096]{0,1:T(8,128)(2,1)S(1)} %fusion.22) | copy-start | bytes 3145732
  61.7 15.2 %collective-permute-start.1 = (bf16[128,4096]{0,1:T(8,128)(2,1)S(1)}, bf16[128,4096]{0,1:T(8,128)(2,1)S(1)}, u32[]{:S(2)}, u32[]{:S(2)}) collective-permute-start(bf16[128,4096]{0,1:T(8,128)(2,1)S(1)} %fusion.30), channel_id=1, source_target_pairs={{0,4},{4,8},{8,12},{12,16},{16,20},{20,24},{24,28},{28,0},{1,5},{5... | collective-permute-start | bytes 3145736 | tf_op jit(solution)/shard_map/ppermute | solution.py:12
  64.4 14.8 %copy-start.8 = (bf16[24,64,64]{2,1,0:T(8,128)(2,1)S(1)}, bf16[24,64,64]{2,1,0:T(8,128)(2,1)}, u32[]{:S(2)}) copy-start(bf16[24,64,64]{2,1,0:T(8,128)(2,1)} %copy-done.6) | copy-start | bytes 589828
  86.2 3.3 %copy-start = (f32[64,128,64]{1,2,0:T(8,128)S(1)}, f32[64,128,64]{1,2,0:T(8,128)}, u32[]{:S(2)}) copy-start(f32[64,128,64]{1,2,0:T(8,128)} %fusion.61) | copy-start | bytes 6291460
  86.2 3.3 %copy-start.24 = (f32[128]{0:T(128)S(1)}, f32[128]{0:T(128)}, u32[]{:S(2)}) copy-start(f32[128]{0:T(128)} %copy-done.23) | copy-start | bytes 1540
  91.4 12.4 %collective-permute-start.3 = (bf16[128,4096]{0,1:T(8,128)(2,1)S(1)}, bf16[128,4096]{0,1:T(8,128)(2,1)S(1)}, u32[]{:S(2)}, u32[]{:S(2)}) collective-permute-start(bf16[128,4096]{0,1:T(8,128)(2,1)S(1)} %fusion.19), channel_id=1, source_target_pairs={{0,28},{4,0},{8,4},{12,8},{16,12},{20,16},{24,20},{28,24},{1,29},{... | collective-permute-start | bytes 3145736 | tf_op jit(solution)/shard_map/ppermute | solution.py:12
  109.1 3.3 %copy-start.1 = (f32[64,128,64]{1,2,0:T(8,128)S(1)}, f32[64,128,64]{1,2,0:T(8,128)}, u32[]{:S(2)}) copy-start(f32[64,128,64]{1,2,0:T(8,128)} %fusion.66) | copy-start | bytes 6291460
  109.1 3.3 %copy-start.22 = (f32[128]{0:T(128)S(1)}, f32[128]{0:T(128)}, u32[]{:S(2)}) copy-start(f32[128]{0:T(128)} %copy-done.21) | copy-start | bytes 1540
  114.2 5.8 %copy-start.5 = (bf16[128,4096]{0,1:T(8,128)(2,1)S(1)}, bf16[128,4096]{0,1:T(8,128)(2,1)}, u32[]{:S(2)}) copy-start(bf16[128,4096]{0,1:T(8,128)(2,1)} %copy-done.4) | copy-start | bytes 3145732
  114.2 15.4 %collective-permute-start.4 = (bf16[128,4096]{0,1:T(8,128)(2,1)}, bf16[128,4096]{0,1:T(8,128)(2,1)}, u32[]{:S(2)}, u32[]{:S(2)}) collective-permute-start(bf16[128,4096]{0,1:T(8,128)(2,1)} %fusion.27), channel_id=1, source_target_pairs={{0,28},{4,0},{8,4},{12,8},{16,12},{20,16},{24,20},{28,24},{1,29},{... | collective-permute-start | bytes 3145736 | tf_op jit(solution)/shard_map/ppermute | solution.py:12
  119.9 9.7 %copy-start.17 = (f32[64,128]{1,0:T(8,128)S(1)}, f32[64,128]{1,0:T(8,128)}, u32[]{:S(2)}) copy-start(f32[64,128]{1,0:T(8,128)} %get-tuple-element.13) | copy-start | bytes 98308
  144.2 30.9 %copy-start.3 = (bf16[128,4096]{0,1:T(8,128)(2,1)S(1)}, bf16[128,4096]{0,1:T(8,128)(2,1)}, u32[]{:S(2)}) copy-start(bf16[128,4096]{0,1:T(8,128)(2,1)} %copy-done.2) | copy-start | bytes 3145732
  171.0 34.8 %all-to-all-start.3 = ((bf16[8,2,6144]{2,1,0:T(2,128)(2,1)}), bf16[8,2,6144]{2,1,0:T(2,128)(2,1)S(1)}, u32[]{:S(2)}, u32[]{:S(2)}) async-start(bf16[8,2,6144]{2,1,0:T(2,128)(2,1)} %reshape.199), calls=%async_computation.3 | async-start | bytes 393216 | tf_op jit(solution)/shard_map/all_to_all | solution.py:105
  181.3 28.7 %copy-start.15 = (f32[4096]{0:T(1024)S(1)}, f32[4096]{0:T(1024)}, u32[]{:S(2)}) copy-start(f32[4096]{0:T(1024)} %get-tuple-element.11) | copy-start | bytes 49156
  181.4 28.6 %copy-start.16 = (f32[4096]{0:T(1024)S(1)}, f32[4096]{0:T(1024)}, u32[]{:S(2)}) copy-start(f32[4096]{0:T(1024)} %get-tuple-element.9) | copy-start | bytes 49156
  205.8 29.7 %all-to-all-start.2 = ((bf16[8,2,6144]{2,1,0:T(2,128)(2,1)}), bf16[8,2,6144]{2,1,0:T(2,128)(2,1)S(1)}, u32[]{:S(2)}, u32[]{:S(2)}) async-start(bf16[8,2,6144]{2,1,0:T(2,128)(2,1)} %reshape.197), calls=%async_computation.2 | async-start | bytes 393216 | tf_op jit(solution)/shard_map/all_to_all | solution.py:98
  (12 other events, 17.0 us)
where the time goes:
time: 242 us; the launch traced here: 241 us
  other arithmetic  68.8 us (28%)
  waiting for transfers between devices  58.5 us (24%)
  matrix products  39 us (16%)
  local copies, waits for them, and re-layouts  32 us (13%)
  starting transfers between devices  22.4 us (9%)
  blocking collectives  19.6 us (8%)
    ppermute x5, waiting for transfers between devices, from_behind(): lax.ppermute(x, axis, [(i, (i + by) % length) for i in range(length)])  50.5 us
    unnamed x3, other arithmetic  47.3 us
    dot_general x17, matrix products, product(): return jnp.einsum(form, left, right, preferred_element_type=jnp.float32)  39 us
    unnamed x66, local copies, waits for them, and re-layouts  20.7 us
    psum x1, blocking collectives, on_device(): gain_summed = lax.psum(gain_total, 'dp')  19.6 us
    reduce_sum x2, other arithmetic, attend_backward(): gain_step = jnp.sum(dquery * unit, axis=0)  6.51 us
    all_to_all x1, waiting for transfers between devices, on_device(): lax.all_to_all(value_rows, 'section', split_axis=1, concat_axis=3, tiled=...  6.05 us
    ppermute x5, starting transfers between devices, from_behind(): lax.ppermute(x, axis, [(i, (i + by) % length) for i in range(length)])  5.55 us
  transfers between devices with their start and end apart: 9, of which 6 were waited for; matrix products, arithmetic and copies ran while one was open for 25% of the time, Pallas kernels for 0%

commit v1 on v0

--- a/solution.py
+++ b/solution.py
@@ -1,3 +1,4 @@
+import functools
 import jax
 import jax.numpy as jnp
 from jax import lax
@@ -5,6 +6,18 @@
 
 HEAD = 64
 TICKS = 3
+
+
+def mix_object_here(point, dimension_no, array_dim):
+    u1 = lax.axis_size("section")
+    aux = jnp.split(point, u1, axis=dimension_no)
+    before = jnp.stack(aux, axis=0)
+    z1 = lax.all_to_all(before, axis_name="section", split_axis=0, concat_axis=0)
+    clean = jnp.concatenate(z1, axis=array_dim)
+    return clean
+
+
+see_scenes_by_axis = functools.partial(mix_object_here, dimension_no=1, array_dim=3)
 
 
 def from_behind(x, axis, by):
@@ -67,7 +80,7 @@
 
 def on_device(inputs, key_rows, value_rows, query_gain, cotangent):
     arrived = (
-        lax.all_to_all(key_rows, "section", split_axis=1, concat_axis=3, tiled=True),
+        see_scenes_by_axis(key_rows),
         lax.all_to_all(value_rows, "section", split_axis=1, concat_axis=3, tiled=True),
     )
     local_keys = arrived[0][0, 0]

time: 242 us -> 256 us (1.058)
  local copies, waits for them, and re-layouts: 32 us -> 42.7 us
    unnamed x66 -> x77, local copies, waits for them, and re-layouts: 20.7 us -> 29.8 us
    all_to_all x1, waiting for transfers between devices: 6.05 us -> 0.01 us  [on_device(): lax.all_to_all(value_rows, 'section', split_axis=1, concat_axis=3, tiled=...]
    all_to_all x1, waiting for transfers between devices: 2.02 us -> 5.89 us  [mix_object_here(): lax.all_to_all(before, axis_name='section', split_axis=0, concat_axis=0)]
  transfers between devices with their start and end apart: 9 -> 9, of which waited for: 6 -> 5; matrix products, arithmetic and copies ran while one was open for 25% -> 28% of each run, Pallas kernels for 0% -> 0%
where the time goes in v1:
time: 256 us; the launch traced here: 254 us
  other arithmetic  69.9 us (27%)
  waiting for transfers between devices  58.2 us (23%)
  local copies, waits for them, and re-layouts  42.7 us (17%)
  matrix products  39.2 us (15%)
  starting transfers between devices  23.4 us (9%)
  blocking collectives  19.6 us (8%)
    ppermute x5, waiting for transfers between devices, from_behind(): lax.ppermute(x, axis, [(i, (i + by) % length) for i in range(length)])  52.4 us
    unnamed x3, other arithmetic  47.3 us
    dot_general x17, matrix products, product(): return jnp.einsum(form, left, right, preferred_element_type=jnp.float32)  39.2 us
    unnamed x77, local copies, waits for them, and re-layouts  29.8 us
    psum x1, blocking collectives, on_device(): gain_summed = lax.psum(gain_total, 'dp')  19.6 us
    reduce_sum x2, other arithmetic, attend_backward(): gain_step = jnp.sum(dquery * unit, axis=0)  6.51 us
    all_to_all x1, waiting for transfers between devices, mix_object_here(): lax.all_to_all(before, axis_name='section', split_axis=0, concat_axis=0)  5.89 us
    ppermute x5, starting transfers between devices, from_behind(): lax.ppermute(x, axis, [(i, (i + by) % length) for i in range(length)])  5.73 us
  transfers between devices with their start and end apart: 9, of which 5 were waited for; matrix products, arithmetic and copies ran while one was open for 28% of the time, Pallas kernels for 0%

profile of v1, /device:TPU:0, one launch (start us, length us, event | category | flops | bytes accessed | tf_op | source)
XLA Modules:
  0.0 254.1 jit_solution(8776048380150414373)
XLA Ops:
  0.6 5.2 %all-to-all-start.1 = ((bf16[1,8,24,512]{3,2,0,1:T(8,128)(2,1)}), bf16[1,8,24,512]{3,2,0,1:T(8,128)(2,1)S(1)}, u32[]{:S(2)}, u32[]{:S(2)}) async-start(bf16[1,8,24,512]{3,2,0,1:T(8,128)(2,1)} %bitcast.156), calls=%async_computation.1 | async-start | bytes 393216 | tf_op jit(solution)/shard_map/all_to_all | solution.py:84
  20.8 4.2 %all-to-all-start = ((bf16[8,1,1,24,512]{4,3,2,1,0:T(8,128)(2,1)}), bf16[8,1,1,24,512]{4,3,2,1,0:T(8,128)(2,1)S(1)}, u32[]{:S(2)}, u32[]{:S(2)}) async-start(bf16[8,1,1,24,512]{4,3,2,1,0:T(8,128)(2,1)} %bitcast_dynamic-update-slice_fusion), calls=%async_computation | async-start | bytes 393216 | tf_op jit(solution)/shard_map/all_to_all | solution.py:15
  25.3 5.9 %all-to-all-done = bf16[8,1,1,24,512]{4,3,2,1,0:T(8,128)(2,1)S(1)} async-done(((bf16[8,1,1,24,512]{4,3,2,1,0:T(8,128)(2,1)}), bf16[8,1,1,24,512]{4,3,2,1,0:T(8,128)(2,1)S(1)}, u32[]{:S(2)}, u32[]{:S(2)}) %all-to-all-start) | async-done | bytes 196640 | tf_op jit(solution)/shard_map/all_to_all | solution.py:15
  42.8 21.3 %collective-permute-done = bf16[128,4096]{0,1:T(8,128)(2,1)S(1)} collective-permute-done((bf16[128,4096]{0,1:T(8,128)(2,1)}, bf16[128,4096]{0,1:T(8,128)(2,1)S(1)}, u32[]{:S(2)}, u32[]{:S(2)}) %collective-permute-start) | collective-permute-done | bytes 1048608 | tf_op jit(solution)/shard_map/ppermute | solution.py:25
  68.5 3.3 %fusion.85 = f32[64,128,64]{1,2,0:T(8,128)} fusion(bf16[24,64,64]{2,1,0:T(8,128)(2,1)S(1)} %reshape_squeeze.2, f32[64,128]{1,0:T(8,128)} %get-tuple-element.15, f32[64,24,128]{2,1,0:T(8,128)} %copy-done.11), kind=kOutput, calls=%fused_computation.105 | convolution fusion | flops 25763864 | bytes 3112960 | tf_op jit(solution)/shard_map/hst,shd->thd/dot_general | solution.py:29
  76.4 12.5 %collective-permute-done.1 = bf16[128,4096]{0,1:T(8,128)(2,1)S(1)} collective-permute-done((bf16[128,4096]{0,1:T(8,128)(2,1)S(1)}, bf16[128,4096]{0,1:T(8,128)(2,1)S(1)}, u32[]{:S(2)}, u32[]{:S(2)}) %collective-permute-start.1) | collective-permute-done | bytes 1048608 | tf_op jit(solution)/shard_map/ppermute | solution.py:25
  94.3 4.1 %fusion.58 = f32[64,64,128]{2,1,0:T(8,128)} fusion(f32[64,24,128]{2,1,0:T(8,128)} %fusion.83, bf16[24,64,64]{2,1,0:T(8,128)(2,1)} %copy-done.6, f32[64,24,128]{2,1,0:T(8,128)} %get-tuple-element.18, f32[64,128]{1,0:T(8,128)} %get-tuple-element.17), kind=kOutput, calls=%fused_computation.78 | convolution fusion | flops 26550296 | bytes 3899392 | tf_op jit(solution)/shard_map/hst,shd->thd/dot_general | solution.py:29
  98.3 3.3 %fusion.20 = (f32[4096]{0:T(1024)}, f32[128]{0:T(128)S(1)}) fusion(bf16[128,4096]{0,1:T(8,128)(2,1)S(1)} %collective-permute-done.1, f32[64,64,128]{2,1,0:T(8,128)} %fusion.58, f32[128]{0:T(128)} %copy-done.25, f32[4096]{0:T(1024)S(1)} %bitcast.146), kind=kLoop, calls=%fused_computation.25 | loop fusion | flops 3665792 | bytes 3179520 | tf_op jit(solution)/shard_map/reduce_sum | solution.py:69
  103.8 12.3 %collective-permute-done.3 = bf16[128,4096]{0,1:T(8,128)(2,1)S(1)} collective-permute-done((bf16[128,4096]{0,1:T(8,128)(2,1)S(1)}, bf16[128,4096]{0,1:T(8,128)(2,1)S(1)}, u32[]{:S(2)}, u32[]{:S(2)}) %collective-permute-start.3) | collective-permute-done | bytes 1048608 | tf_op jit(solution)/shard_map/ppermute | solution.py:25
  117.4 4.1 %fusion.63 = f32[64,64,128]{2,1,0:T(8,128)} fusion(f32[64,24,128]{2,1,0:T(8,128)} %convolution_bitcast_fusion.4, bf16[24,64,64]{2,1,0:T(8,128)(2,1)} %copy-done.6, f32[64,24,128]{2,1,0:T(8,128)} %get-tuple-element.16, f32[64,128]{1,0:T(8,128)} %get-tuple-element.15), kind=kOutput, calls=%fused_computation.82 | convolution fusion | flops 26550296 | bytes 3899392 | tf_op jit(solution)/shard_map/hst,shd->thd/dot_general | solution.py:29
  121.5 3.3 %fusion.28 = (f32[4096]{0:T(1024)}, f32[128]{0:T(128)S(1)}) fusion(bf16[128,4096]{0,1:T(8,128)(2,1)S(1)} %collective-permute-done, f32[64,64,128]{2,1,0:T(8,128)} %fusion.63, f32[128]{0:T(128)} %copy-done.23, f32[4096]{0:T(1024)S(1)} %bitcast.148), kind=kLoop, calls=%fused_computation.33 | loop fusion | flops 3665792 | bytes 3179520 | tf_op jit(solution)/shard_map/reduce_sum | solution.py:69
  132.3 3.4 %fusion.64 = f32[64,64,24]{1,2,0:T(8,128)} fusion(bf16[128,64,64]{0,2,1:T(8,128)(2,1)S(1)} %bitcast.140, f32[64,24,128]{2,1,0:T(8,128)} %convolution_bitcast_fusion.4, f32[64,24,128]{2,1,0:T(8,128)} %get-tuple-element.16, f32[64,128]{1,0:T(8,128)} %get-tuple-element.15), kind=kOutput, calls=%fused_computation.83 | convolution fusion | flops 26550296 | bytes 3047424 | tf_op jit(solution)/shard_map/hst,thd->shd/dot_general | solution.py:29
  135.7 6.2 %collective-permute-done.4 = bf16[128,4096]{0,1:T(8,128)(2,1)} collective-permute-done((bf16[128,4096]{0,1:T(8,128)(2,1)}, bf16[128,4096]{0,1:T(8,128)(2,1)}, u32[]{:S(2)}, u32[]{:S(2)}) %collective-permute-start.4) | collective-permute-done | bytes 1048608 | tf_op jit(solution)/shard_map/ppermute | solution.py:25
  142.0 3.2 %convolution_bitcast_fusion = f32[24,64,64]{2,0,1:T(8,128)} fusion(bf16[128,64,64]{0,2,1:T(8,128)(2,1)} %bitcast.29, f32[64,128]{1,0:T(8,128)S(1)} %copy-done.19, f32[64,24,128]{2,1,0:T(8,128)} %copy-done.15), kind=kOutput, calls=%fused_computation.51 | convolution fusion | flops 25763864 | bytes 2260992 | tf_op jit(solution)/shard_map/hst,thd->shd/dot_general | solution.py:29
  153.4 3.0 %copy.60 = bf16[1,1,24,4096]{2,1,0,3:T(2,128)(2,1)S(1)} copy(bf16[1,1,24,4096]{3,2,1,0:T(8,128)(2,1)S(1)} %convert_element_type.128) | data formatting | bytes 393216 | tf_op jit(solution)/shard_map/convert_element_type | solution.py:119
  156.9 23.5 %reduce.6 = bf16[4096,24]{1,0:T(8,128)(2,1)} reduce(bf16[4096,1,1,24]{3,2,1,0:T(2,128)(2,1)S(1)} %bitcast.133, bf16[]{:T(256)} %broadcast.115), dimensions={1,2}, to_apply=%bitcast.110.reduce_sub_computation | reduce | bytes 393218
  180.4 3.4 %reshape.202 = bf16[8,2,6144]{2,1,0:T(2,128)(2,1)} reshape(bf16[4096,24]{1,0:T(8,128)(2,1)} %reduce.6) | data formatting | bytes 393216
  183.7 4.1 %all-to-all-start.3 = ((bf16[8,2,6144]{2,1,0:T(2,128)(2,1)}), bf16[8,2,6144]{2,1,0:T(2,128)(2,1)S(1)}, u32[]{:S(2)}, u32[]{:S(2)}) async-start(bf16[8,2,6144]{2,1,0:T(2,128)(2,1)} %reshape.202), calls=%async_computation.3 | async-start | bytes 393216 | tf_op jit(solution)/shard_map/all_to_all | solution.py:118
  187.8 3.0 %fusion.57 = bf16[24,64,64]{2,0,1:T(8,128)(2,1)S(1)} fusion(f32[64,64,24]{1,2,0:T(8,128)} %fusion.69, f32[64,64,24]{1,2,0:T(8,128)} %fusion.64, bf16[128,64,64]{0,2,1:T(8,128)(2,1)S(1)} %bitcast.138, f32[64,24,128]{2,1,0:T(8,128)} %fusion.83, f32[64,24,128]{2,1,0:T(8,128)} %get-tuple-element.18, f32[64,128]{1,0:T(8,128)S(1)} %copy-done.20), kind=kOutput, calls=%fused_computation.77 | convolution fusion | flops 26845208 | bytes 3637248 | tf_op jit(solution)/shard_map/hst,thd->shd/dot_general | solution.py:29
  194.0 22.4 %reduce.5 = bf16[4096,24]{1,0:T(8,128)(2,1)S(1)} reduce(bf16[4096,1,1,24]{3,2,1,0:T(2,128)(2,1)S(1)} %bitcast.134, bf16[]{:T(256)} %broadcast.115), dimensions={1,2}, to_apply=%bitcast.108.reduce_sub_computation | reduce | bytes 393218
  218.5 4.2 %all-to-all-start.2 = ((bf16[8,2,6144]{2,1,0:T(2,128)(2,1)}), bf16[8,2,6144]{2,1,0:T(2,128)(2,1)S(1)}, u32[]{:S(2)}, u32[]{:S(2)}) async-start(bf16[8,2,6144]{2,1,0:T(2,128)(2,1)} %reshape.200), calls=%async_computation.2 | async-start | bytes 393216 | tf_op jit(solution)/shard_map/all_to_all | solution.py:111
  222.7 19.6 %psum.7 = f32[1,4096]{1,0:T(1,128)} all-reduce(f32[1,4096]{1,0:T(1,128)S(1)} %bitcast.157), channel_id=1, replica_groups=mesh['section'=8,'dp'=4] {'dp'}, use_global_device_ids=true, to_apply=%region_17.0 | all-reduce | flops 4096 | bytes 32768 | tf_op jit(solution)/shard_map/psum | solution.py:126
  242.3 3.0 %reshape.203 = bf16[4096,1,1,24]{3,2,1,0:T(2,128)(2,1)S(1)} reshape(bf16[8,2,6144]{2,1,0:T(2,128)(2,1)S(1)} %all-to-all-done.3) | data formatting | bytes 393216
  248.2 3.0 %reshape.201 = bf16[4096,1,1,24]{3,2,1,0:T(2,128)(2,1)S(1)} reshape(bf16[8,2,6144]{2,1,0:T(2,128)(2,1)S(1)} %all-to-all-done.2) | data formatting | bytes 393216
  (127 shorter events, 71.7 us)
Async XLA Ops:
  0.6 20.2 %all-to-all-start.1 = ((bf16[1,8,24,512]{3,2,0,1:T(8,128)(2,1)}), bf16[1,8,24,512]{3,2,0,1:T(8,128)(2,1)S(1)}, u32[]{:S(2)}, u32[]{:S(2)}) async-start(bf16[1,8,24,512]{3,2,0,1:T(8,128)(2,1)} %bitcast.156), calls=%async_computation.1 | async-start | bytes 393216 | tf_op jit(solution)/shard_map/all_to_all | solution.py:84
  7.8 23.7 %copy-start.21 = (f32[64,64]{1,0:T(8,128)}, f32[64,64]{1,0:T(8,128)S(1)}, u32[]{:S(2)}) copy-start(f32[64,64]{1,0:T(8,128)S(1)} %mul.89) | copy-start | bytes 49156
  20.8 10.4 %all-to-all-start = ((bf16[8,1,1,24,512]{4,3,2,1,0:T(8,128)(2,1)}), bf16[8,1,1,24,512]{4,3,2,1,0:T(8,128)(2,1)S(1)}, u32[]{:S(2)}, u32[]{:S(2)}) async-start(bf16[8,1,1,24,512]{4,3,2,1,0:T(8,128)(2,1)} %bitcast_dynamic-update-slice_fusion), calls=%async_computation | async-start | bytes 393216 | tf_op jit(solution)/shard_map/all_to_all | solution.py:15
  25.0 7.2 %copy-start.27 = (f32[128]{0:T(128)}, f32[128]{0:T(128)S(1)}, u32[]{:S(2)}) copy-start(f32[128]{0:T(128)S(1)} %add_rsqrt_fusion.2) | copy-start | bytes 1540
  31.5 4.5 %copy-start.6 = (bf16[24,64,64]{2,1,0:T(8,128)(2,1)}, bf16[24,64,64]{2,1,0:T(8,128)(2,1)S(1)}, u32[]{:S(2)}) copy-start(bf16[24,64,64]{2,1,0:T(8,128)(2,1)S(1)} %reshape_squeeze_reshape.2) | copy-start | bytes 589828
  38.9 25.9 %copy-start.13 = (f32[1,4096]{1,0:T(1,128)S(1)}, f32[1,4096]{1,0:T(1,128)}, u32[]{:S(2)}) copy-start(f32[1,4096]{1,0:T(1,128)} %param.8) | copy-start | bytes 49156
  38.9 25.3 %collective-permute-start = (bf16[128,4096]{0,1:T(8,128)(2,1)}, bf16[128,4096]{0,1:T(8,128)(2,1)S(1)}, u32[]{:S(2)}, u32[]{:S(2)}) collective-permute-start(bf16[128,4096]{0,1:T(8,128)(2,1)} %fusion.31), channel_id=1, source_target_pairs={{0,4},{4,8},{8,12},{12,16},{16,20},{20,24},{24,28},{28,0},{1,5},{5... | collective-permute-start | bytes 3145736 | tf_op jit(solution)/shard_map/ppermute | solution.py:25
  40.2 25.3 %copy-start.7 = (bf16[24,64,64]{2,1,0:T(8,128)(2,1)S(1)}, bf16[24,64,64]{2,1,0:T(8,128)(2,1)}, u32[]{:S(2)}) copy-start(bf16[24,64,64]{2,1,0:T(8,128)(2,1)} %copy-done.6) | copy-start | bytes 589828
  40.2 33.6 %collective-permute-start.2 = (bf16[128,4096]{0,1:T(8,128)(2,1)}, bf16[128,4096]{0,1:T(8,128)(2,1)}, u32[]{:S(2)}, u32[]{:S(2)}) collective-permute-start(bf16[128,4096]{0,1:T(8,128)(2,1)} %bitcast.143), channel_id=1, source_target_pairs={{0,28},{4,0},{8,4},{12,8},{16,12},{20,16},{24,20},{28,24},{1,29},{... | collective-permute-start | bytes 3145736 | tf_op jit(solution)/shard_map/ppermute | solution.py:25
  65.5 6.4 %copy-start.4 = (bf16[128,4096]{0,1:T(8,128)(2,1)}, bf16[128,4096]{0,1:T(8,128)(2,1)S(1)}, u32[]{:S(2)}) copy-start(bf16[128,4096]{0,1:T(8,128)(2,1)S(1)} %fusion.22) | copy-start | bytes 3145732
  73.7 15.2 %collective-permute-start.1 = (bf16[128,4096]{0,1:T(8,128)(2,1)S(1)}, bf16[128,4096]{0,1:T(8,128)(2,1)S(1)}, u32[]{:S(2)}, u32[]{:S(2)}) collective-permute-start(bf16[128,4096]{0,1:T(8,128)(2,1)S(1)} %fusion.30), channel_id=1, source_target_pairs={{0,4},{4,8},{8,12},{12,16},{16,20},{20,24},{24,28},{28,0},{1,5},{5... | collective-permute-start | bytes 3145736 | tf_op jit(solution)/shard_map/ppermute | solution.py:25
  76.4 14.8 %copy-start.8 = (bf16[24,64,64]{2,1,0:T(8,128)(2,1)S(1)}, bf16[24,64,64]{2,1,0:T(8,128)(2,1)}, u32[]{:S(2)}) copy-start(bf16[24,64,64]{2,1,0:T(8,128)(2,1)} %copy-done.6) | copy-start | bytes 589828
  98.3 3.3 %copy-start = (f32[64,64,128]{2,1,0:T(8,128)S(1)}, f32[64,64,128]{2,1,0:T(8,128)}, u32[]{:S(2)}) copy-start(f32[64,64,128]{2,1,0:T(8,128)} %fusion.58) | copy-start | bytes 6291460
  98.3 3.3 %copy-start.26 = (f32[128]{0:T(128)S(1)}, f32[128]{0:T(128)}, u32[]{:S(2)}) copy-start(f32[128]{0:T(128)} %copy-done.25) | copy-start | bytes 1540
  103.5 12.6 %collective-permute-start.3 = (bf16[128,4096]{0,1:T(8,128)(2,1)S(1)}, bf16[128,4096]{0,1:T(8,128)(2,1)S(1)}, u32[]{:S(2)}, u32[]{:S(2)}) collective-permute-start(bf16[128,4096]{0,1:T(8,128)(2,1)S(1)} %fusion.19), channel_id=1, source_target_pairs={{0,28},{4,0},{8,4},{12,8},{16,12},{20,16},{24,20},{28,24},{1,29},{... | collective-permute-start | bytes 3145736 | tf_op jit(solution)/shard_map/ppermute | solution.py:25
  121.5 3.3 %copy-start.24 = (f32[128]{0:T(128)S(1)}, f32[128]{0:T(128)}, u32[]{:S(2)}) copy-start(f32[128]{0:T(128)} %copy-done.23) | copy-start | bytes 1540
  126.5 5.8 %copy-start.5 = (bf16[128,4096]{0,1:T(8,128)(2,1)S(1)}, bf16[128,4096]{0,1:T(8,128)(2,1)}, u32[]{:S(2)}) copy-start(bf16[128,4096]{0,1:T(8,128)(2,1)} %copy-done.4) | copy-start | bytes 3145732
  126.5 15.4 %collective-permute-start.4 = (bf16[128,4096]{0,1:T(8,128)(2,1)}, bf16[128,4096]{0,1:T(8,128)(2,1)}, u32[]{:S(2)}, u32[]{:S(2)}) collective-permute-start(bf16[128,4096]{0,1:T(8,128)(2,1)} %fusion.27), channel_id=1, source_target_pairs={{0,28},{4,0},{8,4},{12,8},{16,12},{20,16},{24,20},{28,24},{1,29},{... | collective-permute-start | bytes 3145736 | tf_op jit(solution)/shard_map/ppermute | solution.py:25
  132.3 9.7 %copy-start.19 = (f32[64,128]{1,0:T(8,128)S(1)}, f32[64,128]{1,0:T(8,128)}, u32[]{:S(2)}) copy-start(f32[64,128]{1,0:T(8,128)} %copy-done.18) | copy-start | bytes 98308
  156.9 30.9 %copy-start.3 = (bf16[128,4096]{0,1:T(8,128)(2,1)S(1)}, bf16[128,4096]{0,1:T(8,128)(2,1)}, u32[]{:S(2)}) copy-start(bf16[128,4096]{0,1:T(8,128)(2,1)} %copy-done.2) | copy-start | bytes 3145732
  183.7 34.8 %all-to-all-start.3 = ((bf16[8,2,6144]{2,1,0:T(2,128)(2,1)}), bf16[8,2,6144]{2,1,0:T(2,128)(2,1)S(1)}, u32[]{:S(2)}, u32[]{:S(2)}) async-start(bf16[8,2,6144]{2,1,0:T(2,128)(2,1)} %reshape.202), calls=%async_computation.3 | async-start | bytes 393216 | tf_op jit(solution)/shard_map/all_to_all | solution.py:118
  194.0 28.7 %copy-start.16 = (f32[4096]{0:T(1024)S(1)}, f32[4096]{0:T(1024)}, u32[]{:S(2)}) copy-start(f32[4096]{0:T(1024)} %get-tuple-element.11) | copy-start | bytes 49156
  194.0 28.7 %copy-start.17 = (f32[4096]{0:T(1024)S(1)}, f32[4096]{0:T(1024)}, u32[]{:S(2)}) copy-start(f32[4096]{0:T(1024)} %get-tuple-element.9) | copy-start | bytes 49156
  218.5 29.7 %all-to-all-start.2 = ((bf16[8,2,6144]{2,1,0:T(2,128)(2,1)}), bf16[8,2,6144]{2,1,0:T(2,128)(2,1)S(1)}, u32[]{:S(2)}, u32[]{:S(2)}) async-start(bf16[8,2,6144]{2,1,0:T(2,128)(2,1)} %reshape.200), calls=%async_computation.2 | async-start | bytes 393216 | tf_op jit(solution)/shard_map/all_to_all | solution.py:111
  (14 other events, 20.5 us)
